TPU v7x, 256 devices: a whole 4x4x8 slice. The times are simulated.
256 devices in a mesh: row: 8 (over y, core), col: 16 (over z_hi, x), layer: 2 (over z_lo).
Axes of the slice: x: 4, y: 4, z: 8 (z_hi: 4, z_lo: 2; z = z_hi * 2 + z_lo), core: 2. Of those that a mesh axis runs over, the one named last changes fastest.
Arguments:
- tile_values: float32 [8, 32, 2, 6, 128, 128], P('row', ('col', 'layer')), may hold values from -1.8 to 1.8
- tile_rows: int32 [8, 32, 2, 6], P('row', ('col', 'layer')), may hold values from 0 to 255, as said below
- tile_cols: int32 [8, 32, 2, 6], P('row', ('col', 'layer')), may hold values from 0 to 255, as said below
- tile_counts: int32 [8, 32, 2], P('row', ('col', 'layer')), may hold values from 1 to 6, as said below
- out_rows: int32 [8, 16, 2, 12], P('row', 'col'), may hold values from 0 to 255, as said below
- out_cols: int32 [8, 16, 2, 12], P('row', 'col'), may hold values from 0 to 255, as said below
Outputs:
- squared: float32 [8, 32, 12, 128, 128], P('row', ('col', 'layer'))
Inputs may be any that keep to these rules, and one draw needn't show every extreme that they name: `tile_rows`: entry [r, s, h, q] lies in row band r (the 32 block rows from r * 32), in a run of 8 block rows whose index is congruent to h modulo 2; within one list [r, s, h] the 6 slots have distinct rows. `tile_cols`: entry [r, s, h, q] lies in sub-band s: block columns s * 8 to s * 8 + 7. Slots q < tile_counts[r, s, h] of list [r, s, h] hold tiles; values and coordinates in later slots mean nothing. Some list holds 6 tiles in every draw. out_rows[r, c, l, o] and out_cols[r, c, l, o] place the o-th kept tile of row band r and sub-band c * 2 + l; the row lies in row band r, the column in that sub-band, and the 12 positions of one [r, c, l] are distinct. `out_cols`: see out_rows.
All inputs are finite; a program needn't handle non-finite values.
Results may differ from a plain program's by a relative error of at most 0.0003.
Values sent between devices are 32-bit elements; how exact they have to be, the bound alone decides.
No kernel may reach another device: no remote copies, remote signals or barrier semaphores. Data moves between devices by JAX's collectives and lax.ppermute only.
A program may use at most 128 MiB of HBM per device.

v0:
```python
import jax
import jax.numpy as jnp
from jax import lax
from jax.sharding import PartitionSpec as P


def live_slots(counts, capacity):
    slot_ids = jnp.arange(capacity, dtype=jnp.int32)
    return slot_ids < counts[..., None]


def flatten_list(listed):
    values, list_rows, list_cols, counts = listed
    tile_order = values.shape[-1]
    capacity = values.shape[-3]
    live_mask = live_slots(counts, capacity)
    return (
        values.reshape(-1, tile_order, tile_order),
        list_rows.reshape(-1),
        list_cols.reshape(-1),
        live_mask.reshape(-1),
    )


def tile_products(running, one_shard, column_panel, target_rows, target_cols):
    left_values, left_rows, left_cols, left_live = one_shard
    right_values, right_rows, right_cols, right_live = column_panel
    left_hits = (left_live[None, :] & (left_rows[None, :] == target_rows[:, None])).astype(
        jnp.int32
    )
    left_pick = jnp.argmax(left_hits, axis=1)
    inner_index = jnp.take(left_cols, left_pick)
    right_hits = (
        right_live[None, :]
        & (right_rows[None, :] == inner_index[:, None])
        & (right_cols[None, :] == target_cols[:, None])
    ).astype(jnp.int32)
    right_pick = jnp.argmax(right_hits, axis=1)
    weight = (jnp.max(left_hits, axis=1) * jnp.max(right_hits, axis=1)).astype(jnp.float32)
    left_tiles = jnp.take(left_values, left_pick, axis=0)
    right_tiles = jnp.take(right_values, right_pick, axis=0)
    products = jnp.einsum(
        "opq,oqr->opr",
        left_tiles,
        right_tiles,
        precision=lax.Precision.HIGHEST,
        preferred_element_type=jnp.float32,
    )
    return running + products * weight[:, None, None]


def column_panel_of(listed):
    return flatten_list(lax.all_gather(listed, "row", axis=0, tiled=True))


def fold_over(column_panel, target_rows, target_cols, running, arrived):
    values, piece_rows, piece_cols, counts = arrived
    pieces_count = values.shape[1]
    tile_order = values.shape[-1]
    capacity = values.shape[-3]
    live_mask = live_slots(counts, capacity)
    shards = (
        values.reshape(pieces_count, -1, tile_order, tile_order),
        piece_rows.reshape(pieces_count, -1),
        piece_cols.reshape(pieces_count, -1),
        live_mask.reshape(pieces_count, -1),
    )

    def advance(carried, one_shard):
        return (tile_products(carried, one_shard, column_panel, target_rows, target_cols), None)

    running, unused = lax.scan(advance, running, shards)
    return running


def local(tile_values, tile_rows, tile_cols, tile_counts, out_rows, out_cols):
    tile_order = tile_values.shape[-1]
    own_list = (tile_values, tile_rows, tile_cols, tile_counts)
    column_panel = column_panel_of(own_list)
    layer_index = lax.axis_index("layer")
    target_rows = lax.dynamic_index_in_dim(out_rows[0, 0], layer_index, 0, keepdims=False)
    target_cols = lax.dynamic_index_in_dim(out_cols[0, 0], layer_index, 0, keepdims=False)
    empty_sums = jnp.zeros((target_rows.shape[0], tile_order, tile_order), jnp.float32)
    summed = fold_over(
        column_panel,
        target_rows,
        target_cols,
        empty_sums,
        (
            lax.all_gather(own_list[0], ("col", "layer"), axis=1, tiled=True),
            lax.all_gather(own_list[1], ("col", "layer"), axis=1, tiled=True),
            lax.all_gather(own_list[2], ("col", "layer"), axis=1, tiled=True),
            lax.all_gather(own_list[3], ("col", "layer"), axis=1, tiled=True),
        ),
    )
    result = summed.reshape(1, 1, -1, tile_order, tile_order)
    return result


def solution(mesh):
    in_specs = (
        P("row", ("col", "layer"), None, None, None, None),
        P("row", ("col", "layer"), None, None),
        P("row", ("col", "layer"), None, None),
        P("row", ("col", "layer"), None),
        P("row", "col", None, None),
        P("row", "col", None, None),
    )
    out_specs = P("row", ("col", "layer"), None, None, None)
    return jax.shard_map(local, mesh=mesh, in_specs=in_specs, out_specs=out_specs, check_vma=False)
```

profile of v0, /device:TPU:1, one launch (start us, length us, event | category | flops | bytes accessed | tf_op | source)
XLA Modules:
  0.0 899.1 jit_solution(16524936345030754830)
XLA Ops:
  8.0 12.2 %all_gather.27 = s32[8,1,2]{2,1,0:T(1,128)S(1)} all-gather(s32[1,1,2]{2,1,0:T(1,128)} %param.11), channel_id=1, replica_groups=mesh['row'=8,'col'=16,'layer'=2] {'row'}, dimensions={0}, use_global_device_ids=true | all-gather | bytes 72 | tf_op jit(solution)/shard_map/all_gather | solution.py:53
  20.2 8.8 all_gather.30
  29.1 9.3 %all_gather.28 = s32[8,1,2,6]{3,2,1,0:T(2,128)S(1)} all-gather(s32[1,1,2,6]{3,2,1,0:T(2,128)} %param.9), channel_id=1, replica_groups=mesh['row'=8,'col'=16,'layer'=2] {'row'}, dimensions={0}, use_global_device_ids=true | all-gather | bytes 432 | tf_op jit(solution)/shard_map/all_gather | solution.py:53
  38.5 64.3 %all_gather.25 = s32[1,32,2,6]{3,2,0,1:T(2,128)S(1)} all-gather(s32[1,1,2,6]{3,2,0,1:T(2,128)} %bitcast.52), channel_id=1, replica_groups=mesh['row'=8,'col'=16,'layer'=2] {'col','layer'}, dimensions={1}, use_global_device_ids=true | all-gather | bytes 1584 | tf_op jit(solution)/shard_map/all_gather | solution.py:91
  103.0 58.1 %all_gather.29 = s32[1,32,2,6]{3,2,0,1:T(2,128)S(1)} all-gather(s32[1,1,2,6]{3,2,0,1:T(2,128)} %bitcast.53), channel_id=1, replica_groups=mesh['row'=8,'col'=16,'layer'=2] {'col','layer'}, dimensions={1}, use_global_device_ids=true | all-gather | bytes 1584 | tf_op jit(solution)/shard_map/all_gather | solution.py:92
  161.2 57.5 %all_gather.24 = s32[1,32,2]{2,0,1:T(1,128)S(1)} all-gather(s32[1,1,2]{2,0,1:T(1,128)} %bitcast.55), channel_id=1, replica_groups=mesh['row'=8,'col'=16,'layer'=2] {'col','layer'}, dimensions={1}, use_global_device_ids=true | all-gather | bytes 264 | tf_op jit(solution)/shard_map/all_gather | solution.py:93
  219.7 377.2 %all-gather.3.cloned.1.call-done = f32[1,32,2,6,128,128]{5,4,3,2,0,1:T(8,128)} async-done(((f32[1,1,2,6,128,128]{5,4,3,2,0,1:T(8,128)}), f32[1,32,2,6,128,128]{5,4,3,2,0,1:T(8,128)}) %all-gather.3.cloned.1.call-update) | async-done | bytes 25165840 | tf_op jit(solution)/shard_map/all_gather | solution.py:90
  596.9 294.5 %while.12 = (s32[]{:T(128)}, f32[12,128,128]{2,1,0:T(8,128)S(1)}, pred[32,12]{1,0:T(8,128)(4,1)S(1)}, s32[32,12]{1,0:T(8,128)S(1)}, s32[12]{0:T(128)S(1)}, /*ind...) while((s32[]{:T(128)}, f32[12,128,128]{2,1,0:T(8,128)S(1)}, ...), condition=%wide.wide.region_5.6_spmd.clone, body=%wide.wide.region_0.5_spmd.clone.sunk | while | flops 302997888 | bytes 7876635 | solution.py:72
  599.3 3.4 gather_fusion.1
  608.5 3.4 gather_fusion.1
  612.3 1.2 dynamic-slice_bitcast_fusion.9
  617.8 3.4 gather_fusion.1
  627.0 3.4 gather_fusion.1
  630.7 1.2 dynamic-slice_bitcast_fusion.9
  636.2 3.4 gather_fusion.1
  645.4 3.4 gather_fusion.1
  649.2 1.2 dynamic-slice_bitcast_fusion.9
  654.6 3.4 gather_fusion.1
  663.8 3.4 gather_fusion.1
  667.6 1.2 dynamic-slice_bitcast_fusion.9
  673.0 3.4 gather_fusion.1
  676.8 1.2 dynamic-slice_bitcast_fusion.9
  682.2 3.4 gather_fusion.1
  686.0 1.2 dynamic-slice_bitcast_fusion.9
  691.4 3.4 gather_fusion.1
  695.2 1.2 dynamic-slice_bitcast_fusion.9
  700.6 3.4 gather_fusion.1
  704.4 1.2 dynamic-slice_bitcast_fusion.9
  709.8 3.4 gather_fusion.1
  719.0 3.4 gather_fusion.1
  728.2 3.4 gather_fusion.1
  737.4 3.4 gather_fusion.1
  746.6 3.4 gather_fusion.1
  755.8 3.4 gather_fusion.1
  765.0 3.4 gather_fusion.1
  774.2 3.4 gather_fusion.1
  783.4 3.4 gather_fusion.1
  792.6 3.4 gather_fusion.1
  801.8 3.4 gather_fusion.1
  811.0 3.4 gather_fusion.1
  820.2 3.4 gather_fusion.1
  829.4 3.4 gather_fusion.1
  838.7 3.4 gather_fusion.1
  847.9 3.4 gather_fusion.1
  857.1 3.4 gather_fusion.1
  866.3 3.4 gather_fusion.1
  875.5 3.4 gather_fusion.1
  884.7 3.4 gather_fusion.1
  (624 shorter events, 178.0 us)
Async XLA Ops:
  6.5 213.2 %all-gather.5.cloned.1.call-start = ((), (), s32[]{:S(2)}) async-start(), calls=%async_computation.1 | async-start | bytes 7077888 | tf_op jit(solution)/shard_map/all_gather | solution.py:53
  7.3 589.6 %all-gather.3.cloned.1.call-start = ((), (), s32[]{:S(2)}) async-start(), calls=%async_computation | async-start | bytes 25952256 | tf_op jit(solution)/shard_map/all_gather | solution.py:90
  29.0 567.9 %copy-start.1 = (s32[8,1,2,6]{3,2,1,0:T(2,128)}, s32[8,1,2,6]{3,2,1,0:T(2,128)S(1)}, u32[]{:S(2)}) copy-start(s32[8,1,2,6]{3,2,1,0:T(2,128)S(1)} %all_gather.30) | copy-start | bytes 1156
  38.4 558.5 %copy-start.2 = (s32[8,1,2,6]{3,2,1,0:T(2,128)}, s32[8,1,2,6]{3,2,1,0:T(2,128)S(1)}, u32[]{:S(2)}) copy-start(s32[8,1,2,6]{3,2,1,0:T(2,128)S(1)} %all_gather.28) | copy-start | bytes 1156
  891.4 0.9 copy-start
Sparse Core Ops, SparseCore 0:
  9.2 47.7 all-gather.4
  58.8 538.0 all-gather.2
where the time goes:
time: 902 us; the launch traced here: 899 us
  waiting for transfers between devices  379 us (42%)
  blocking collectives  210 us (23%)
  local copies, waits for them, and re-layouts  193 us (21%)
  other arithmetic  65.1 us (7%)
  matrix products  36.4 us (4%)
  between operations  13.4 us (1%)
    all_gather x1, waiting for transfers between devices, local(): lax.all_gather(own_list[0], ('col', 'layer'), axis=1, tiled=True)  377 us
    gather x32, local copies, waits for them, and re-layouts, tile_products(): right_tiles = jnp.take(right_values, right_pick, axis=0)  108 us
    all_gather x1, blocking collectives, local(): lax.all_gather(own_list[1], ('col', 'layer'), axis=1, tiled=True)  64.3 us
    all_gather x1, blocking collectives, local(): lax.all_gather(own_list[2], ('col', 'layer'), axis=1, tiled=True)  58.1 us
    all_gather x1, blocking collectives, local(): lax.all_gather(own_list[3], ('col', 'layer'), axis=1, tiled=True)  57.5 us
    squeeze x32, local copies, waits for them, and re-layouts, fold_over(): running, unused = lax.scan(advance, running, shards)  38.1 us
    dot_general x32, matrix products, tile_products(): jnp.einsum('opq,oqr->opr', left_tiles, right_tiles, precision=lax.Precisi...  36.4 us
    all_gather x3, blocking collectives, column_panel_of(): return flatten_list(lax.all_gather(listed, 'row', axis=0, tiled=True))  30.3 us
  transfers between devices with their start and end apart: 2, of which 1 were waited for; matrix products, arithmetic and copies ran while one was open for 0% of the time, Pallas kernels for 0%

commit v1 on v0

--- a/solution.py
+++ b/solution.py
@@ -89,7 +89,15 @@
         (
             lax.all_gather(own_list[0], ("col", "layer"), axis=1, tiled=True),
             lax.all_gather(own_list[1], ("col", "layer"), axis=1, tiled=True),
-            lax.all_gather(own_list[2], ("col", "layer"), axis=1, tiled=True),
+            jnp.concatenate(
+                jax.lax.all_to_all(
+                    jnp.stack(jax.lax.axis_size(("col", "layer")) * [own_list[2]]),
+                    ("col", "layer"),
+                    0,
+                    0,
+                ),
+                axis=1,
+            ),
             lax.all_gather(own_list[3], ("col", "layer"), axis=1, tiled=True),
         ),
     )

time: 902 us -> 897 us (level)
  blocking collectives: 210 us -> 161 us
  waiting for transfers between devices: 379 us -> 414 us
  starting transfers between devices: 0.04 us -> 11.9 us
    all_gather x1 -> x0, blocking collectives: 58.1 us -> none  [local(): lax.all_gather(own_list[2], ('col', 'layer'), axis=1, tiled=True)]
    all_gather x1, waiting for transfers between devices: 377 us -> 413 us  [local(): lax.all_gather(own_list[0], ('col', 'layer'), axis=1, tiled=True)]
    all_gather x3, blocking collectives: 30.3 us -> 43.4 us  [column_panel_of(): return flatten_list(lax.all_gather(listed, 'row', axis=0, tiled=True))]
    all_to_all x0 -> x1, starting transfers between devices: none -> 11.9 us  [local(): jax.lax.all_to_all(jnp.stack(jax.lax.axis_size(('col', 'layer')) * [own_l...]
  transfers between devices with their start and end apart: 2 -> 3, of which waited for: 1 -> 1; matrix products, arithmetic and copies ran while one was open for 0% -> 0% of each run, Pallas kernels for 0% -> 0%
where the time goes in v1:
time: 897 us; the launch traced here: 894 us
  waiting for transfers between devices  414 us (46%)
  local copies, waits for them, and re-layouts  194 us (22%)
  blocking collectives  161 us (18%)
  other arithmetic  60.9 us (7%)
  matrix products  36.4 us (4%)
  between operations  13.4 us (1%)
  starting transfers between devices  11.9 us (1%)
    all_gather x1, waiting for transfers between devices, local(): lax.all_gather(own_list[0], ('col', 'layer'), axis=1, tiled=True)  413 us
    gather x32, local copies, waits for them, and re-layouts, tile_products(): right_tiles = jnp.take(right_values, right_pick, axis=0)  108 us
    all_gather x1, blocking collectives, local(): lax.all_gather(own_list[3], ('col', 'layer'), axis=1, tiled=True)  59.4 us
    all_gather x1, blocking collectives, local(): lax.all_gather(own_list[1], ('col', 'layer'), axis=1, tiled=True)  58.2 us
    all_gather x3, blocking collectives, column_panel_of(): return flatten_list(lax.all_gather(listed, 'row', axis=0, tiled=True))  43.4 us
    squeeze x32, local copies, waits for them, and re-layouts, fold_over(): running, unused = lax.scan(advance, running, shards)  38.1 us
    dot_general x32, matrix products, tile_products(): jnp.einsum('opq,oqr->opr', left_tiles, right_tiles, precision=lax.Precisi...  36.4 us
    another operation x32, other arithmetic, tile_products(): right_pick = jnp.argmax(right_hits, axis=1)  22.5 us
  transfers between devices with their start and end apart: 3, of which 1 were waited for; matrix products, arithmetic and copies ran while one was open for 0% of the time, Pallas kernels for 0%

profile of v1, /device:TPU:1, one launch (start us, length us, event | category | flops | bytes accessed | tf_op | source)
XLA Modules:
  0.0 894.3 jit_solution(4937947733133689669)
XLA Ops:
  8.0 1.3 stack.2
  9.3 11.9 %all-to-all-start = ((s32[32,1,1,2,6]{4,3,2,1,0:T(2,128)}), s32[32,1,1,2,6]{4,3,2,1,0:T(2,128)S(1)}, u32[]{:S(2)}, u32[]{:S(2)}) async-start(s32[32,1,1,2,6]{4,3,2,1,0:T(2,128)} %stack.2), calls=%async_computation | async-start | bytes 65536 | tf_op jit(solution)/shard_map/all_to_all | solution.py:93
  21.2 59.4 %all_gather.21 = s32[1,32,2]{2,0,1:T(1,128)S(1)} all-gather(s32[1,1,2]{2,0,1:T(1,128)} %bitcast.53), channel_id=1, replica_groups=mesh['row'=8,'col'=16,'layer'=2] {'col','layer'}, dimensions={1}, use_global_device_ids=true | all-gather | bytes 264 | tf_op jit(solution)/shard_map/all_gather | solution.py:101
  81.5 25.3 %all_gather.24 = s32[8,1,2]{2,1,0:T(1,128)S(1)} all-gather(s32[1,1,2]{2,1,0:T(1,128)} %param.11), channel_id=1, replica_groups=mesh['row'=8,'col'=16,'layer'=2] {'row'}, dimensions={0}, use_global_device_ids=true | all-gather | bytes 72 | tf_op jit(solution)/shard_map/all_gather | solution.py:53
  106.8 8.4 all_gather.26
  115.3 9.8 %all_gather.25 = s32[8,1,2,6]{3,2,1,0:T(2,128)S(1)} all-gather(s32[1,1,2,6]{3,2,1,0:T(2,128)} %param.9), channel_id=1, replica_groups=mesh['row'=8,'col'=16,'layer'=2] {'row'}, dimensions={0}, use_global_device_ids=true | all-gather | bytes 432 | tf_op jit(solution)/shard_map/all_gather | solution.py:53
  125.1 58.2 %all_gather.22 = s32[1,32,2,6]{3,2,0,1:T(2,128)S(1)} all-gather(s32[1,1,2,6]{3,2,0,1:T(2,128)} %bitcast.51), channel_id=1, replica_groups=mesh['row'=8,'col'=16,'layer'=2] {'col','layer'}, dimensions={1}, use_global_device_ids=true | all-gather | bytes 1584 | tf_op jit(solution)/shard_map/all_gather | solution.py:91
  183.6 412.7 %all-gather.3.cloned.1.call-done = f32[1,32,2,6,128,128]{5,4,3,2,0,1:T(8,128)} async-done(((f32[1,1,2,6,128,128]{5,4,3,2,0,1:T(8,128)}), f32[1,32,2,6,128,128]{5,4,3,2,0,1:T(8,128)}) %all-gather.3.cloned.1.call-update) | async-done | bytes 25165840 | tf_op jit(solution)/shard_map/all_gather | solution.py:90
  596.3 290.3 %while.12 = (s32[]{:T(128)}, f32[12,128,128]{2,1,0:T(8,128)S(1)}, pred[32,12]{1,0:T(8,128)(4,1)S(1)}, s32[32,12]{1,0:T(8,128)S(1)}, s32[12]{0:T(128)S(1)}, /*ind...) while((s32[]{:T(128)}, f32[12,128,128]{2,1,0:T(8,128)S(1)}, ...), condition=%wide.wide.region_5.6_spmd.clone, body=%wide.wide.region_0.5_spmd.clone.sunk | while | flops 302997888 | bytes 7876635 | solution.py:72
  598.6 3.4 gather_fusion.1
  602.4 1.2 dynamic-slice_bitcast_fusion.9
  607.6 3.4 gather_fusion.1
  616.7 3.4 gather_fusion.1
  620.5 1.2 dynamic-slice_bitcast_fusion.9
  625.8 3.4 gather_fusion.1
  629.6 1.2 dynamic-slice_bitcast_fusion.9
  634.9 3.4 gather_fusion.1
  643.9 3.4 gather_fusion.1
  647.7 1.2 dynamic-slice_bitcast_fusion.9
  653.0 3.4 gather_fusion.1
  662.1 3.4 gather_fusion.1
  665.9 1.2 dynamic-slice_bitcast_fusion.9
  671.2 3.4 gather_fusion.1
  674.9 1.2 dynamic-slice_bitcast_fusion.9
  680.2 3.4 gather_fusion.1
  684.0 1.2 dynamic-slice_bitcast_fusion.9
  689.3 3.4 gather_fusion.1
  698.4 3.4 gather_fusion.1
  707.4 3.4 gather_fusion.1
  716.5 3.4 gather_fusion.1
  725.6 3.4 gather_fusion.1
  734.7 3.4 gather_fusion.1
  743.7 3.4 gather_fusion.1
  752.8 3.4 gather_fusion.1
  761.9 3.4 gather_fusion.1
  771.0 3.4 gather_fusion.1
  780.0 3.4 gather_fusion.1
  789.1 3.4 gather_fusion.1
  798.2 3.4 gather_fusion.1
  807.2 3.4 gather_fusion.1
  816.3 3.4 gather_fusion.1
  825.4 3.4 gather_fusion.1
  834.5 3.4 gather_fusion.1
  843.5 3.4 gather_fusion.1
  852.6 3.4 gather_fusion.1
  861.7 3.4 gather_fusion.1
  870.8 3.4 gather_fusion.1
  879.8 3.4 gather_fusion.1
  (626 shorter events, 175.0 us)
Async XLA Ops:
  6.5 177.0 %all-gather.5.cloned.1.call-start = ((), (), s32[]{:S(2)}) async-start(), calls=%async_computation.2 | async-start | bytes 7077888 | tf_op jit(solution)/shard_map/all_gather | solution.py:53
  7.3 589.0 %all-gather.3.cloned.1.call-start = ((), (), s32[]{:S(2)}) async-start(), calls=%async_computation.1 | async-start | bytes 25952256 | tf_op jit(solution)/shard_map/all_gather | solution.py:90
  9.3 174.2 %all-to-all-start = ((s32[32,1,1,2,6]{4,3,2,1,0:T(2,128)}), s32[32,1,1,2,6]{4,3,2,1,0:T(2,128)S(1)}, u32[]{:S(2)}, u32[]{:S(2)}) async-start(s32[32,1,1,2,6]{4,3,2,1,0:T(2,128)} %stack.2), calls=%async_computation | async-start | bytes 65536 | tf_op jit(solution)/shard_map/all_to_all | solution.py:93
  115.2 481.1 %copy-start.1 = (s32[8,1,2,6]{3,2,1,0:T(2,128)}, s32[8,1,2,6]{3,2,1,0:T(2,128)S(1)}, u32[]{:S(2)}) copy-start(s32[8,1,2,6]{3,2,1,0:T(2,128)S(1)} %all_gather.26) | copy-start | bytes 1156
  125.0 471.2 %copy-start.2 = (s32[8,1,2,6]{3,2,1,0:T(2,128)}, s32[8,1,2,6]{3,2,1,0:T(2,128)S(1)}, u32[]{:S(2)}) copy-start(s32[8,1,2,6]{3,2,1,0:T(2,128)S(1)} %all_gather.25) | copy-start | bytes 1156
  886.6 0.9 copy-start
Sparse Core Ops, SparseCore 0:
  9.2 47.6 all-gather.4
  58.7 537.4 all-gather.2
